TPU v7x, 128 devices: a whole 4x4x4 slice. The times are simulated.
128 devices in a mesh: gx: 16 (over y, x), gy: 8 (over z, core).
Axes of the slice: x: 4, y: 4, z: 4, core: 2. Of those that a mesh axis runs over, the one named last changes fastest.
Arguments:
- prior_member_matrix: float32 [8, 256, 256, 128], P(None, 'gx', 'gy'), may hold values from -6 to 6
- east_speed: float32 [4, 256, 256], P(None, 'gx', 'gy'), may hold values from -0.3 to 0.3
- north_speed: float32 [4, 256, 256], P(None, 'gx', 'gy'), may hold values from -0.3 to 0.3
- diffusion: float32 [4, 256, 256], P(None, 'gx', 'gy'), may hold values from 0.1 to 0.22
- obs_column: int32 [1024, 2], replicated, may hold values from 0 to 255, as said below
- obs_comp: int32 [1024], replicated, may hold values from 0 to 7
- observation_reach: int32 [1024], replicated, may hold values from 0 to 3
- obs_owner: int32 [1024], replicated, may hold values from 0 to 15, as said below
- obs_order: int32 [1024], replicated, may hold values from 0 to 1023, each once
- obs_value: float32 [16, 8, 32], P('gx', 'gy'), may hold values from -6 to 6
- obs_error: float32 [16, 8, 32], P('gx', 'gy'), may hold values from 0.3 to 3
Outputs:
- analysis: float32 [8, 256, 256, 128], P(None, 'gx', 'gy')
Inputs may be any that keep to these rules, and one draw needn't show every extreme that they name: `obs_column`: tile t = (8 tx + ty) holds observations 8 t to 8 (t + 1) - 1; each entry is a (longitude, latitude) column inside that tile. `obs_owner`: the owner lies in the observation's latitude tile; one tile's observations reach one owner at most 2 times, and exactly 2 times for some owner of every tile.
All inputs are finite; a program needn't handle non-finite values.
Results may differ from a plain program's by a relative error of at most 0.0001.
Values sent between devices are 32-bit elements; how exact they have to be, the bound alone decides.
No kernel may reach another device: no remote copies, remote signals or barrier semaphores. Data moves between devices by JAX's collectives and lax.ppermute only.
A program may use at most 64 MiB of HBM per device.

v0:
```python
import jax
import jax.numpy as jnp
from jax import lax
from jax.sharding import PartitionSpec as P

FSTEPS = 2
PANEL = 256
PRECISE = lax.Precision.HIGHEST


def with_halo(cells, sides, width, closed):
    for axis, dim in sides:
        count = lax.axis_size(axis)
        ends = count if closed else count - 1
        head = lax.slice_in_dim(cells, 0, width, axis=dim)
        tail = lax.slice_in_dim(cells, cells.shape[dim] - width, cells.shape[dim], axis=dim)
        cells = jnp.concatenate(
            [
                lax.ppermute(tail, axis, [(i, (i + 1) % count) for i in range(ends)]),
                cells,
                lax.ppermute(head, axis, [((i + 1) % count, i) for i in range(ends)]),
            ],
            axis=dim,
        )
    return cells


def slot_rank(tile_x, tile_y, owner, tiles_x, tiles_y):
    total_obs = owner.shape[0]
    keyed = (tile_x * tiles_y + tile_y) * tiles_x + owner
    sort_order = jnp.argsort(keyed, stable=True)
    sorted_keys = keyed[sort_order]
    places = jnp.arange(total_obs, dtype=jnp.int32)
    segment_beginning = jnp.concatenate(
        [jnp.ones((1,), dtype=bool), sorted_keys[1:] != sorted_keys[:-1]]
    )
    starts = lax.cummax(jnp.where(segment_beginning, places, 0), axis=0)
    ranked = places - starts
    inverse_order = jnp.argsort(sort_order)
    return ranked[inverse_order]


def horizontal(first_x, first_y, second_x, second_y, span_x, span_y, total_x):
    wrapped = (first_x - second_x) % total_x
    dist_x = jnp.minimum(wrapped, total_x - wrapped).astype(jnp.float32)
    dist_y = (first_y - second_y).astype(jnp.float32)
    radius_sq = (dist_x / span_x) ** 2 + (dist_y / span_y) ** 2
    return jnp.maximum(0.0, 1.0 - radius_sq) ** 2


def vertical(first_level, second_level, reach):
    level_gap = jnp.abs(first_level - second_level).astype(jnp.float32)
    return jnp.maximum(0.0, 1.0 - level_gap / (reach.astype(jnp.float32) + 1.0))


def panel_terms(priors, values, errors):
    members = priors.shape[1]
    centre = jnp.mean(priors, axis=1)
    spread = priors - centre[:, None]
    variance = jnp.sum(spread * spread, axis=1) / (members - 1)
    inverse = 1.0 / (variance + errors)
    damping = 1.0 / (1.0 + jnp.sqrt(errors * inverse))
    return (spread, (values - centre) * inverse, damping * inverse)


def regress(row_block, weight, spread, mean_gain, shrink):
    members = row_block.shape[1]
    centre = jnp.mean(row_block, axis=1, keepdims=True)
    anomaly = row_block - centre
    covariance = jnp.dot(
        anomaly, spread.T, precision=PRECISE, preferred_element_type=jnp.float32
    ) / (members - 1)
    weighted = weight * covariance
    centre = centre + jnp.dot(
        weighted, mean_gain[:, None], precision=PRECISE, preferred_element_type=jnp.float32
    )
    anomaly = anomaly - jnp.dot(
        weighted * shrink[None, :], spread, precision=PRECISE, preferred_element_type=jnp.float32
    )
    return centre + anomaly


def shards(
    prior_member_matrix,
    east_speed,
    north_speed,
    diffusion,
    obs_column,
    obs_comp,
    observation_reach,
    obs_owner,
    obs_order,
    obs_value,
    obs_error,
):
    comps, zonal_extent, width_y, members = prior_member_matrix.shape
    per_level = comps // east_speed.shape[0]
    tiles_x = lax.axis_size("gx")
    tiles_y = lax.axis_size("gy")
    here_x = lax.axis_index("gx")
    here_y = lax.axis_index("gy")
    east_vel = jnp.repeat(east_speed, per_level, axis=0)[..., None]
    north_vel = jnp.repeat(north_speed, per_level, axis=0)[..., None]
    diff_coef = jnp.repeat(diffusion, per_level, axis=0)[..., None]
    model_mesh_values = prior_member_matrix
    for substep in range(FSTEPS):
        rim_wide = with_halo(model_mesh_values, (("gx", 1),), 1, True)
        rim_tall = with_halo(model_mesh_values, (("gy", 2),), 1, False)
        east_side = rim_wide[:, 2:]
        west_side = rim_wide[:, :-2]
        north_side = rim_tall[:, :, 2:]
        south_side = rim_tall[:, :, :-2]
        spread_term = diff_coef * (
            east_side + west_side + north_side + south_side - 4.0 * model_mesh_values
        )
        carry_term = 0.5 * (
            east_vel * (east_side - west_side) + north_vel * (north_side - south_side)
        )
        model_mesh_values = model_mesh_values + spread_term - carry_term
    row_state = model_mesh_values.reshape(comps * zonal_extent * width_y, members)
    obs_total = obs_comp.shape[0]
    slot_count = obs_value.shape[2]
    capacity = slot_count // tiles_x
    panel_count = obs_total // PANEL
    col_x = obs_column[:, 0]
    col_y = obs_column[:, 1]
    tile_x = col_x // zonal_extent
    tile_y = col_y // width_y
    ranked_slot = slot_rank(tile_x, tile_y, obs_owner, tiles_x, tiles_y)
    obs_level = obs_comp // per_level
    in_tile = (tile_x == here_x) & (tile_y == here_y)
    held_here = (obs_owner == here_x) & (tile_y == here_y)
    own_place = tile_x * capacity + ranked_slot
    element = (
        (obs_comp * zonal_extent + col_x - tile_x * zonal_extent) * width_y
        + col_y
        - tile_y * width_y
    )
    total_x = zonal_extent * tiles_x
    grid_x = jnp.repeat(here_x * zonal_extent + jnp.arange(zonal_extent, dtype=jnp.int32), width_y)
    grid_y = jnp.tile(here_y * width_y + jnp.arange(width_y, dtype=jnp.int32), zonal_extent)
    comp_level = jnp.arange(comps, dtype=jnp.int32) // per_level
    local_vals = obs_value.reshape(slot_count)
    local_errs = obs_error.reshape(slot_count)

    def state_weight(panel_index_list):
        flat_weight = horizontal(
            grid_x[:, None],
            grid_y[:, None],
            col_x[panel_index_list][None, :],
            col_y[panel_index_list][None, :],
            3.0 * zonal_extent,
            3.0 * width_y,
            total_x,
        )
        level_weight = vertical(
            comp_level[:, None],
            obs_level[panel_index_list][None, :],
            observation_reach[panel_index_list][None, :],
        )
        return (level_weight[:, None, :] * flat_weight[None, :, :]).reshape(
            -1, panel_index_list.shape[0]
        )

    slot_ids = jnp.arange(slot_count, dtype=jnp.int32)
    measurement_labels = jnp.arange(obs_total, dtype=jnp.int32)
    send_place = obs_owner * capacity + ranked_slot
    send_match = in_tile[None, :] & (send_place[None, :] == slot_ids[:, None])
    filled = jnp.any(send_match, axis=1)
    source_elem = jnp.sum(jnp.where(send_match, element[None, :], 0), axis=1)
    outgoing = jnp.where(filled[:, None], row_state[source_elem], 0.0).reshape(
        tiles_x, capacity, members
    )
    arrived = lax.all_to_all(outgoing, "gx", split_axis=0, concat_axis=0, tiled=True).reshape(
        slot_count, members
    )
    hold_match = held_here[None, :] & (own_place[None, :] == slot_ids[:, None])
    held_obs = jnp.sum(jnp.where(hold_match, measurement_labels[None, :], 0), axis=1)
    slot_east_coord = col_x[held_obs]
    slot_y = col_y[held_obs]
    slot_level = obs_level[held_obs]
    all_vals, all_errs = (
        lax.all_gather(local_vals, ("gx", "gy"), axis=0, tiled=True),
        lax.all_gather(local_errs, ("gx", "gy"), axis=0, tiled=True),
    )
    global_place = (obs_owner * tiles_y + tile_y) * slot_count + own_place
    obs_vals = all_vals[global_place]
    obs_errs = all_errs[global_place]

    def one_panel(panel_num, carried):
        row_state, owner_rows = carried
        panel_index_list = lax.dynamic_slice_in_dim(obs_order, panel_num * PANEL, PANEL)
        every_slot = lax.all_gather(owner_rows, ("gx", "gy"), axis=0, tiled=True)
        priors = every_slot[global_place[panel_index_list]]
        spread, mean_gain, shrink = panel_terms(
            priors, obs_vals[panel_index_list], obs_errs[panel_index_list]
        )
        owner_weight = horizontal(
            slot_east_coord[:, None],
            slot_y[:, None],
            col_x[panel_index_list][None, :],
            col_y[panel_index_list][None, :],
            3.0 * zonal_extent,
            3.0 * width_y,
            total_x,
        )
        owner_weight = owner_weight * vertical(
            slot_level[:, None],
            obs_level[panel_index_list][None, :],
            observation_reach[panel_index_list][None, :],
        )
        new_state = regress(row_state, state_weight(panel_index_list), spread, mean_gain, shrink)
        new_owner = regress(owner_rows, owner_weight, spread, mean_gain, shrink)
        return (new_state, new_owner)

    row_state, owner_rows = lax.fori_loop(0, panel_count, one_panel, (row_state, arrived))
    return row_state.reshape(comps, zonal_extent, width_y, members)


def solution(mesh):
    return jax.shard_map(
        shards,
        mesh=mesh,
        in_specs=(
            P(None, "gx", "gy", None),
            P(None, "gx", "gy"),
            P(None, "gx", "gy"),
            P(None, "gx", "gy"),
            P(),
            P(),
            P(),
            P(),
            P(),
            P("gx", "gy", None),
            P("gx", "gy", None),
        ),
        out_specs=P(None, "gx", "gy", None),
        check_vma=False,
    )
```

profile of v0, /device:TPU:1, one launch (start us, length us, event | category | flops | bytes accessed | tf_op | source)
XLA Modules:
  0.0 494.7 jit_solution(18060016406997314425)
XLA Ops:
  7.8 3.3 collective-permute-start.2
  11.2 3.5 collective-permute-start.3
  17.0 3.8 collective-permute-start
  23.0 4.4 sort.34
  27.4 4.5 gather_fusion.8
  32.0 4.4 sort.35
  37.0 4.5 gather_fusion.9
  43.7 64.4 %all-reduce.2 = (f32[4096]{0:T(1024)S(1)}, f32[4096]{0:T(1024)S(1)}) all-reduce(f32[4096]{0:T(1024)S(1)} %bitcast_dynamic-update-slice_fusion.1, f32[4096]{0:T(1024)S(1)} %bitcast_dynamic-update-slice_fusion), channel_id=2, replica_groups=mesh['gx'=16,'gy'=8] {'gx','gy'}, use_global_device_ids=true, to_apply=%add | all-reduce | flops 8192 | bytes 65536 | tf_op jit(solution)/shard_map/all_gather | solution.py:183
  108.0 6.1 %gather_fusion.12 = f32[1024]{0:T(1024)S(1)} fusion(f32[4096]{0:T(1024)S(1)} %get-tuple-element.561, s32[1024]{0:T(1024)S(1)} %get-tuple-element.564), kind=kCustom, calls=%fused_computation.12 | custom fusion | bytes 12288 | tf_op jit(solution)/shard_map/gather | solution.py:188
  114.2 6.2 %gather_fusion.11 = f32[1024]{0:T(1024)S(1)} fusion(f32[4096]{0:T(1024)S(1)} %get-tuple-element.560, s32[1024]{0:T(1024)S(1)} %get-tuple-element.564), kind=kCustom, calls=%fused_computation.11 | custom fusion | bytes 12288 | tf_op jit(solution)/shard_map/gather | solution.py:187
  123.9 4.5 collective-permute-start.4
  128.5 3.1 collective-permute-start.6
  131.6 2.5 collective-permute-start.7
  138.8 3.5 all-to-all-start
  142.9 5.8 %all-to-all-done = f32[16,2,128]{2,1,0:T(2,128)S(1)} async-done(((f32[16,2,128]{2,1,0:T(2,128)}), f32[16,2,128]{2,1,0:T(2,128)S(1)}, u32[]{:S(2)}, u32[]{:S(2)}) %all-to-all-start) | async-done | bytes 16416 | tf_op jit(solution)/shard_map/all_to_all | solution.py:174
  148.7 338.1 %while.18 = (s32[]{:T(128)}, f32[4096,128]{1,0:T(8,128)S(1)}, f32[32,128]{1,0:T(8,128)S(1)}, s32[1024]{0:T(1024)}, s32[1024]{0:T(1024)S(1)}, /*index=5*/s32[1024...) while((s32[]{:T(128)}, f32[4096,128]{1,0:T(8,128)S(1)}, ...), condition=%wide.region_12.13_spmd.clone, body=%wide.region_7.12_spmd.clone.sunk | while | flops 3269761536 | bytes 36260832 | solution.py:216
  163.8 54.0 %all-gather.4.cloned.1.call-done = f32[4096,128]{1,0:T(8,128)} async-done(((f32[32,128]{1,0:T(8,128)}), f32[4096,128]{1,0:T(8,128)}) %all-gather.4.cloned.1.call-update) | async-done | bytes 2097168 | tf_op jit(solution)/shard_map/while/body/eval_jaxpr/all_gather | solution.py:193
  220.9 5.6 %fusion.99 = f32[4096,256]{1,0:T(8,128)S(1)} fusion(f32[4096,256]{1,0:T(8,128)} %bitcast.72, f32[4096,128]{1,0:T(8,128)S(1)} %get-tuple-element.720, f32[4096]{0:T(1024)S(1)} %broadcast_multiply_fusion.10, f32[256,128]{1,0:T(8,128)S(1)} %gather_fusion.1, f32[256]{0:T(256)S(1)} %broadcast_multiply_fusion.8), kind=kOutput, calls=%fused_computation.20.clone.1 | convolution fusion | flops 1613266944 | bytes 10634240 | tf_op jit(solution)/shard_map/while/body/eval_jaxpr/dot_general | solution.py:70
  226.5 3.6 fusion.100
  230.4 4.6 fusion.102
  250.3 51.6 %all-gather.4.cloned.1.call-done = f32[4096,128]{1,0:T(8,128)} async-done(((f32[32,128]{1,0:T(8,128)}), f32[4096,128]{1,0:T(8,128)}) %all-gather.4.cloned.1.call-update) | async-done | bytes 2097168 | tf_op jit(solution)/shard_map/while/body/eval_jaxpr/all_gather | solution.py:193
  305.0 5.6 %fusion.99 = f32[4096,256]{1,0:T(8,128)S(1)} fusion(f32[4096,256]{1,0:T(8,128)} %bitcast.72, f32[4096,128]{1,0:T(8,128)S(1)} %get-tuple-element.720, f32[4096]{0:T(1024)S(1)} %broadcast_multiply_fusion.10, f32[256,128]{1,0:T(8,128)S(1)} %gather_fusion.1, f32[256]{0:T(256)S(1)} %broadcast_multiply_fusion.8), kind=kOutput, calls=%fused_computation.20.clone.1 | convolution fusion | flops 1613266944 | bytes 10634240 | tf_op jit(solution)/shard_map/while/body/eval_jaxpr/dot_general | solution.py:70
  310.5 3.6 fusion.100
  314.5 4.6 fusion.102
  334.3 51.6 %all-gather.4.cloned.1.call-done = f32[4096,128]{1,0:T(8,128)} async-done(((f32[32,128]{1,0:T(8,128)}), f32[4096,128]{1,0:T(8,128)}) %all-gather.4.cloned.1.call-update) | async-done | bytes 2097168 | tf_op jit(solution)/shard_map/while/body/eval_jaxpr/all_gather | solution.py:193
  389.0 5.6 %fusion.99 = f32[4096,256]{1,0:T(8,128)S(1)} fusion(f32[4096,256]{1,0:T(8,128)} %bitcast.72, f32[4096,128]{1,0:T(8,128)S(1)} %get-tuple-element.720, f32[4096]{0:T(1024)S(1)} %broadcast_multiply_fusion.10, f32[256,128]{1,0:T(8,128)S(1)} %gather_fusion.1, f32[256]{0:T(256)S(1)} %broadcast_multiply_fusion.8), kind=kOutput, calls=%fused_computation.20.clone.1 | convolution fusion | flops 1613266944 | bytes 10634240 | tf_op jit(solution)/shard_map/while/body/eval_jaxpr/dot_general | solution.py:70
  394.6 3.6 fusion.100
  398.5 4.6 fusion.102
  418.2 51.4 %all-gather.4.cloned.1.call-done = f32[4096,128]{1,0:T(8,128)} async-done(((f32[32,128]{1,0:T(8,128)}), f32[4096,128]{1,0:T(8,128)}) %all-gather.4.cloned.1.call-update) | async-done | bytes 2097168 | tf_op jit(solution)/shard_map/while/body/eval_jaxpr/all_gather | solution.py:193
  472.7 5.6 %fusion.99 = f32[4096,256]{1,0:T(8,128)S(1)} fusion(f32[4096,256]{1,0:T(8,128)} %bitcast.72, f32[4096,128]{1,0:T(8,128)S(1)} %get-tuple-element.720, f32[4096]{0:T(1024)S(1)} %broadcast_multiply_fusion.10, f32[256,128]{1,0:T(8,128)S(1)} %gather_fusion.1, f32[256]{0:T(256)S(1)} %broadcast_multiply_fusion.8), kind=kOutput, calls=%fused_computation.20.clone.1 | convolution fusion | flops 1613266944 | bytes 10634240 | tf_op jit(solution)/shard_map/while/body/eval_jaxpr/dot_general | solution.py:70
  478.3 3.6 fusion.100
  482.2 4.6 fusion.102
  (226 shorter events, 92.2 us)
Async XLA Ops:
  7.8 113.3 %collective-permute-start.2 = (f32[8,16,1,128]{3,2,1,0:T(1,128)S(1)}, f32[8,16,1,128]{3,2,1,0:T(1,128)S(1)}, u32[]{:S(2)}, u32[]{:S(2)}) collective-permute-start(f32[8,16,1,128]{3,2,1,0:T(1,128)S(1)} %get-tuple-element.577), channel_id=1, source_target_pairs={{1,0},{2,1},{3,2},{4,3},{5,4},{6,5},{7,6},{9,8},{10,9},{11,10},{12... | collective-permute-start | bytes 196616 | tf_op jit(solution)/shard_map/ppermute | solution.py:21
  11.2 110.0 %collective-permute-start.3 = (f32[8,16,1,128]{3,2,1,0:T(1,128)S(1)}, f32[8,16,1,128]{3,2,1,0:T(1,128)S(1)}, u32[]{:S(2)}, u32[]{:S(2)}) collective-permute-start(f32[8,16,1,128]{3,2,1,0:T(1,128)S(1)} %get-tuple-element.578), channel_id=1, source_target_pairs={{0,1},{1,2},{2,3},{3,4},{4,5},{5,6},{6,7},{8,9},{9,10},{10,11},{11... | collective-permute-start | bytes 196616 | tf_op jit(solution)/shard_map/ppermute | solution.py:19
  15.7 105.5 %collective-permute-start.1 = (f32[8,1,32,128]{3,2,1,0:T(8,128)S(1)}, f32[8,1,32,128]{3,2,1,0:T(8,128)S(1)}, u32[]{:S(2)}, u32[]{:S(2)}) collective-permute-start(f32[8,1,32,128]{3,2,1,0:T(8,128)S(1)} %get-tuple-element.575), channel_id=1, source_target_pairs={{0,8},{8,16},{16,24},{24,32},{32,40},{40,48},{48,56},{56,64},{64,7... | collective-permute-start | bytes 393224 | tf_op jit(solution)/shard_map/ppermute | solution.py:19
  17.0 104.2 %collective-permute-start = (f32[8,1,32,128]{3,2,1,0:T(8,128)S(1)}, f32[8,1,32,128]{3,2,1,0:T(8,128)S(1)}, u32[]{:S(2)}, u32[]{:S(2)}) collective-permute-start(f32[8,1,32,128]{3,2,1,0:T(8,128)S(1)} %get-tuple-element.576), channel_id=1, source_target_pairs={{8,0},{16,8},{24,16},{32,24},{40,32},{48,40},{56,48},{64,56},{72,6... | collective-permute-start | bytes 393224 | tf_op jit(solution)/shard_map/ppermute | solution.py:21
  37.0 4.6 copy-start.5
  37.0 4.6 copy-start.9
  37.0 5.0 %copy-start.10 = (f32[1,1,32]{2,1,0:T(1,128)S(1)}, f32[1,1,32]{2,1,0:T(1,128)}, u32[]{:S(2)}) copy-start(f32[1,1,32]{2,1,0:T(1,128)} %param.22) | copy-start | bytes 388
  37.0 5.2 %copy-start.11 = (f32[1,1,32]{2,1,0:T(1,128)S(1)}, f32[1,1,32]{2,1,0:T(1,128)}, u32[]{:S(2)}) copy-start(f32[1,1,32]{2,1,0:T(1,128)} %param.23) | copy-start | bytes 388
  114.2 7.0 %copy-start.6 = (f32[4,16,32]{2,1,0:T(8,128)S(1)}, f32[4,16,32]{2,1,0:T(8,128)}, u32[]{:S(2)}) copy-start(f32[4,16,32]{2,1,0:T(8,128)} %param.14) | copy-start | bytes 24580
  114.2 7.0 %copy-start.7 = (f32[4,16,32]{2,1,0:T(8,128)S(1)}, f32[4,16,32]{2,1,0:T(8,128)}, u32[]{:S(2)}) copy-start(f32[4,16,32]{2,1,0:T(8,128)} %param.15) | copy-start | bytes 24580
  114.2 7.1 %copy-start.8 = (f32[4,16,32]{2,1,0:T(8,128)S(1)}, f32[4,16,32]{2,1,0:T(8,128)}, u32[]{:S(2)}) copy-start(f32[4,16,32]{2,1,0:T(8,128)} %param.16) | copy-start | bytes 24580
  114.2 7.1 %copy-start.4 = (f32[8,16,32,128]{3,2,1,0:T(8,128)S(1)}, f32[8,16,32,128]{3,2,1,0:T(8,128)}, u32[]{:S(2)}) copy-start(f32[8,16,32,128]{3,2,1,0:T(8,128)} %param.13) | copy-start | bytes 6291460
  123.6 11.8 %collective-permute-start.5 = (f32[8,1,32,128]{3,2,1,0:T(8,128)S(1)}, f32[8,1,32,128]{3,2,1,0:T(8,128)S(1)}, u32[]{:S(2)}, u32[]{:S(2)}) collective-permute-start(f32[8,1,32,128]{3,2,1,0:T(8,128)S(1)} %get-tuple-element.571), channel_id=1, source_target_pairs={{0,8},{8,16},{16,24},{24,32},{32,40},{40,48},{48,56},{56,64},{64,7... | collective-permute-start | bytes 393224 | tf_op jit(solution)/shard_map/ppermute | solution.py:19
  123.9 11.5 %collective-permute-start.4 = (f32[8,1,32,128]{3,2,1,0:T(8,128)S(1)}, f32[8,1,32,128]{3,2,1,0:T(8,128)S(1)}, u32[]{:S(2)}, u32[]{:S(2)}) collective-permute-start(f32[8,1,32,128]{3,2,1,0:T(8,128)S(1)} %get-tuple-element.572), channel_id=1, source_target_pairs={{8,0},{16,8},{24,16},{32,24},{40,32},{48,40},{56,48},{64,56},{72,6... | collective-permute-start | bytes 393224 | tf_op jit(solution)/shard_map/ppermute | solution.py:21
  128.5 5.6 %collective-permute-start.6 = (f32[8,16,1,128]{3,2,1,0:T(1,128)S(1)}, f32[8,16,1,128]{3,2,1,0:T(1,128)S(1)}, u32[]{:S(2)}, u32[]{:S(2)}) collective-permute-start(f32[8,16,1,128]{3,2,1,0:T(1,128)S(1)} %get-tuple-element.573), channel_id=1, source_target_pairs={{1,0},{2,1},{3,2},{4,3},{5,4},{6,5},{7,6},{9,8},{10,9},{11,10},{12... | collective-permute-start | bytes 196616 | tf_op jit(solution)/shard_map/ppermute | solution.py:21
  131.6 3.8 collective-permute-start.7
  137.6 11.2 %copy-start = (s32[1024]{0:T(1024)S(1)}, s32[1024]{0:T(1024)}, u32[]{:S(2)}) copy-start(s32[1024]{0:T(1024)} %param.19) | copy-start | bytes 12292
  138.8 9.9 %all-to-all-start = ((f32[16,2,128]{2,1,0:T(2,128)}), f32[16,2,128]{2,1,0:T(2,128)S(1)}, u32[]{:S(2)}, u32[]{:S(2)}) async-start(f32[16,2,128]{2,1,0:T(2,128)} %broadcast_select_fusion), calls=%async_computation | async-start | bytes 32768 | tf_op jit(solution)/shard_map/all_to_all | solution.py:174
  148.7 0.6 copy-start.2
  148.7 69.1 %all-gather.4.cloned.1.call-start = ((), (), s32[]{:S(2)}) async-start(), calls=%async_computation.1 | async-start | bytes 2113536 | tf_op jit(solution)/shard_map/while/body/eval_jaxpr/all_gather | solution.py:193
  161.5 58.9 %copy-start.3 = (f32[32,128]{1,0:T(8,128)S(1)}, f32[32,128]{1,0:T(8,128)}, u32[]{:S(2)}) copy-start(f32[32,128]{1,0:T(8,128)} %copy-done.2) | copy-start | bytes 49156 | tf_op jit(solution)/shard_map/while
  235.1 0.6 copy-start.2
  235.1 66.8 %all-gather.4.cloned.1.call-start = ((), (), s32[]{:S(2)}) async-start(), calls=%async_computation.1 | async-start | bytes 2113536 | tf_op jit(solution)/shard_map/while/body/eval_jaxpr/all_gather | solution.py:193
  247.9 56.6 %copy-start.3 = (f32[32,128]{1,0:T(8,128)S(1)}, f32[32,128]{1,0:T(8,128)}, u32[]{:S(2)}) copy-start(f32[32,128]{1,0:T(8,128)} %copy-done.2) | copy-start | bytes 49156 | tf_op jit(solution)/shard_map/while
  319.1 0.6 copy-start.2
  319.1 66.8 %all-gather.4.cloned.1.call-start = ((), (), s32[]{:S(2)}) async-start(), calls=%async_computation.1 | async-start | bytes 2113536 | tf_op jit(solution)/shard_map/while/body/eval_jaxpr/all_gather | solution.py:193
  332.0 56.6 %copy-start.3 = (f32[32,128]{1,0:T(8,128)S(1)}, f32[32,128]{1,0:T(8,128)}, u32[]{:S(2)}) copy-start(f32[32,128]{1,0:T(8,128)} %copy-done.2) | copy-start | bytes 49156 | tf_op jit(solution)/shard_map/while
  403.1 0.6 copy-start.2
  403.2 66.4 %all-gather.4.cloned.1.call-start = ((), (), s32[]{:S(2)}) async-start(), calls=%async_computation.1 | async-start | bytes 2113536 | tf_op jit(solution)/shard_map/while/body/eval_jaxpr/all_gather | solution.py:193
  415.9 56.4 %copy-start.3 = (f32[32,128]{1,0:T(8,128)S(1)}, f32[32,128]{1,0:T(8,128)}, u32[]{:S(2)}) copy-start(f32[32,128]{1,0:T(8,128)} %copy-done.2) | copy-start | bytes 49156 | tf_op jit(solution)/shard_map/while
  486.8 1.3 copy-start.1
Sparse Core Ops, SparseCore 0:
  152.7 65.1 all-gather.3
  239.1 62.7 all-gather.3
  323.1 62.7 all-gather.3
  406.8 62.7 all-gather.3
where the time goes:
time: 496 us; the launch traced here: 495 us
  waiting for transfers between devices  216 us (44%)
  local copies, waits for them, and re-layouts  79.7 us (16%)
  blocking collectives  64.4 us (13%)
  matrix products  58.2 us (12%)
  other arithmetic  36.2 us (7%)
  starting transfers between devices  26 us (5%)
  between operations  13.4 us (3%)
    all_gather x4, waiting for transfers between devices, one_panel(): every_slot = lax.all_gather(owner_rows, ('gx', 'gy'), axis=0, tiled=True)  209 us
    all_gather x1, blocking collectives, shards(): lax.all_gather(local_vals, ('gx', 'gy'), axis=0, tiled=True)  64.4 us
    dot_general x8, matrix products, regress(): jnp.dot(anomaly, spread.T, precision=PRECISE, preferred_element_type=jnp....  23.6 us
    dot_general x8, matrix products, regress(): jnp.dot(weighted * shrink[None, :], spread, precision=PRECISE, preferred_...  19.7 us
    dot_general x8, matrix products, regress(): jnp.dot(weighted, mean_gain[:, None], precision=PRECISE, preferred_elemen...  15 us
    gather x8, local copies, waits for them, and re-layouts, one_panel(): priors = every_slot[global_place[panel_index_list]]  14.7 us
    ppermute x4, starting transfers between devices, with_halo(): lax.ppermute(head, axis, [((i + 1) % count, i) for i in range(ends)])  14.7 us
  transfers between devices with their start and end apart: 13, of which 6 were waited for; matrix products, arithmetic and copies ran while one was open for 19% of the time, Pallas kernels for 0%

commit v1 on v0

--- a/solution.py
+++ b/solution.py
@@ -190,7 +190,12 @@
     def one_panel(panel_num, carried):
         row_state, owner_rows = carried
         panel_index_list = lax.dynamic_slice_in_dim(obs_order, panel_num * PANEL, PANEL)
-        every_slot = lax.all_gather(owner_rows, ("gx", "gy"), axis=0, tiled=True)
+        every_slot = jnp.concatenate(
+            lax.all_to_all(
+                jnp.stack([owner_rows] * lax.axis_size(("gx", "gy"))), ("gx", "gy"), 0, 0
+            ),
+            axis=0,
+        )
         priors = every_slot[global_place[panel_index_list]]
         spread, mean_gain, shrink = panel_terms(
             priors, obs_vals[panel_index_list], obs_errs[panel_index_list]

time: 496 us -> 365 us (0.74)
  waiting for transfers between devices: 216 us -> 72.3 us
  starting transfers between devices: 26 us -> 51.3 us
  between operations: 13.4 us -> 0.37 us
    all_gather x4 -> x0, waiting for transfers between devices: 209 us -> none  [one_panel(): every_slot = lax.all_gather(owner_rows, ('gx', 'gy'), axis=0, tiled=True)]
    all_to_all x0 -> x4, waiting for transfers between devices: none -> 65.2 us  [one_panel(): lax.all_to_all(jnp.stack([owner_rows] * lax.axis_size(('gx', 'gy'))), ('g...]
    all_to_all x0 -> x4, starting transfers between devices: none -> 25.4 us  [one_panel(): lax.all_to_all(jnp.stack([owner_rows] * lax.axis_size(('gx', 'gy'))), ('g...]
    another operation x1 -> x5, local copies, waits for them, and re-layouts: 0.12 us -> 6.44 us  [the longest x4 6.32 us: one_panel(): jnp.stack([owner_rows] * lax.axis_size(('gx', 'gy')))]
  transfers between devices with their start and end apart: 13 -> 13, of which waited for: 6 -> 6; matrix products, arithmetic and copies ran while one was open for 19% -> 25% of each run, Pallas kernels for 0% -> 0%
where the time goes in v1:
time: 365 us; the launch traced here: 364 us
  local copies, waits for them, and re-layouts  83.8 us (23%)
  waiting for transfers between devices  72.3 us (20%)
  blocking collectives  64.4 us (18%)
  matrix products  58.2 us (16%)
  starting transfers between devices  51.3 us (14%)
  other arithmetic  33.3 us (9%)
    all_to_all x4, waiting for transfers between devices, one_panel(): lax.all_to_all(jnp.stack([owner_rows] * lax.axis_size(('gx', 'gy'))), ('g...  65.2 us
    all_gather x1, blocking collectives, shards(): lax.all_gather(local_vals, ('gx', 'gy'), axis=0, tiled=True)  64.4 us
    all_to_all x4, starting transfers between devices, one_panel(): lax.all_to_all(jnp.stack([owner_rows] * lax.axis_size(('gx', 'gy'))), ('g...  25.4 us
    dot_general x8, matrix products, regress(): jnp.dot(anomaly, spread.T, precision=PRECISE, preferred_element_type=jnp....  23.6 us
    dot_general x8, matrix products, regress(): jnp.dot(weighted * shrink[None, :], spread, precision=PRECISE, preferred_...  19.7 us
    dot_general x8, matrix products, regress(): jnp.dot(weighted, mean_gain[:, None], precision=PRECISE, preferred_elemen...  15 us
    gather x8, local copies, waits for them, and re-layouts, one_panel(): priors = every_slot[global_place[panel_index_list]]  14.7 us
    ppermute x4, starting transfers between devices, with_halo(): lax.ppermute(head, axis, [((i + 1) % count, i) for i in range(ends)])  14.7 us
  transfers between devices with their start and end apart: 13, of which 6 were waited for; matrix products, arithmetic and copies ran while one was open for 25% of the time, Pallas kernels for 0%

profile of v1, /device:TPU:1, one launch (start us, length us, event | category | flops | bytes accessed | tf_op | source)
XLA Modules:
  0.0 364.2 jit_solution(5253012108497954847)
XLA Ops:
  4.6 3.5 collective-permute-start.3
  10.5 3.8 %collective-permute-start = (f32[8,1,32,128]{3,2,1,0:T(8,128)S(1)}, f32[8,1,32,128]{3,2,1,0:T(8,128)S(1)}, u32[]{:S(2)}, u32[]{:S(2)}) collective-permute-start(f32[8,1,32,128]{3,2,1,0:T(8,128)S(1)} %get-tuple-element.576), channel_id=1, source_target_pairs={{8,0},{16,8},{24,16},{32,24},{40,32},{48,40},{56,48},{64,56},{72,6... | collective-permute-start | bytes 393224 | tf_op jit(solution)/shard_map/ppermute | solution.py:21
  16.5 4.4 %sort.34 = (s32[1024]{0:T(1024)}, s32[1024]{0:T(1024)S(1)}) sort(s32[1024]{0:T(1024)S(1)} %multiply_add_fusion.2, s32[1024]{0:T(1024)S(1)} %iota.44), dimensions={0}, to_apply=%region_0.1 | sort | flops 10240 | bytes 16384 | tf_op jit(solution)/shard_map/jit(argsort)/sort | solution.py:31
  20.8 4.5 %gather_fusion.8 = s32[1024]{0:T(1024)S(1)} fusion(s32[1024]{0:T(1024)S(1)} %multiply_add_fusion.2, s32[1024]{0:T(1024)S(1)} %fusion.51), kind=kCustom, calls=%fused_computation.8 | custom fusion | bytes 12288 | tf_op jit(solution)/shard_map/gather | solution.py:32
  25.5 4.4 %sort.35 = (s32[1024]{0:T(1024)}, s32[1024]{0:T(1024)S(1)}) sort(s32[1024]{0:T(1024)S(1)} %get-tuple-element.404, s32[1024]{0:T(1024)S(1)} %iota.50), dimensions={0}, to_apply=%region_3.4 | sort | flops 10240 | bytes 16384 | tf_op jit(solution)/shard_map/jit(argsort)/sort | solution.py:39
  30.5 4.5 %gather_fusion.9 = s32[1024]{0:T(1024)S(1)} fusion(s32[1024]{0:T(1024)S(1)} %get-tuple-element.585, s32[1024]{0:T(1024)S(1)} %get-tuple-element.584), kind=kCustom, calls=%fused_computation.9 | custom fusion | bytes 12288 | tf_op jit(solution)/shard_map/gather | solution.py:40
  37.1 64.4 %all-reduce.2 = (f32[4096]{0:T(1024)S(1)}, f32[4096]{0:T(1024)S(1)}) all-reduce(f32[4096]{0:T(1024)S(1)} %bitcast_dynamic-update-slice_fusion.1, f32[4096]{0:T(1024)S(1)} %bitcast_dynamic-update-slice_fusion), channel_id=2, replica_groups=mesh['gx'=16,'gy'=8] {'gx','gy'}, use_global_device_ids=true, to_apply=%add | all-reduce | flops 8192 | bytes 65536 | tf_op jit(solution)/shard_map/all_gather | solution.py:183
  101.5 6.1 %gather_fusion.12 = f32[1024]{0:T(1024)S(1)} fusion(f32[4096]{0:T(1024)S(1)} %get-tuple-element.561, s32[1024]{0:T(1024)S(1)} %get-tuple-element.564), kind=kCustom, calls=%fused_computation.12 | custom fusion | bytes 12288 | tf_op jit(solution)/shard_map/gather | solution.py:188
  107.7 6.2 %gather_fusion.11 = f32[1024]{0:T(1024)S(1)} fusion(f32[4096]{0:T(1024)S(1)} %get-tuple-element.560, s32[1024]{0:T(1024)S(1)} %get-tuple-element.564), kind=kCustom, calls=%fused_computation.11 | custom fusion | bytes 12288 | tf_op jit(solution)/shard_map/gather | solution.py:187
  117.4 4.5 %collective-permute-start.4 = (f32[8,1,32,128]{3,2,1,0:T(8,128)S(1)}, f32[8,1,32,128]{3,2,1,0:T(8,128)S(1)}, u32[]{:S(2)}, u32[]{:S(2)}) collective-permute-start(f32[8,1,32,128]{3,2,1,0:T(8,128)S(1)} %get-tuple-element.572), channel_id=1, source_target_pairs={{8,0},{16,8},{24,16},{32,24},{40,32},{48,40},{56,48},{64,56},{72,6... | collective-permute-start | bytes 393224 | tf_op jit(solution)/shard_map/ppermute | solution.py:21
  136.4 5.8 %all-to-all-done.1 = f32[16,2,128]{2,1,0:T(2,128)S(1)} async-done(((f32[16,2,128]{2,1,0:T(2,128)}), f32[16,2,128]{2,1,0:T(2,128)S(1)}, u32[]{:S(2)}, u32[]{:S(2)}) %all-to-all-start.1) | async-done | bytes 16416 | tf_op jit(solution)/shard_map/all_to_all | solution.py:174
  142.2 220.7 %while.18 = (s32[]{:T(128)}, f32[4096,128]{1,0:T(8,128)S(1)}, f32[32,128]{1,0:T(8,128)S(1)}, s32[1024]{0:T(1024)}, s32[1024]{0:T(1024)S(1)}, /*index=5*/s32[1024...) while((s32[]{:T(128)}, f32[4096,128]{1,0:T(8,128)S(1)}, ...), condition=%wide.region_12.13_spmd.clone, body=%wide.region_7.12_spmd.clone.sunk | while | flops 3269761536 | bytes 38194076 | solution.py:221
  143.8 8.1 %all-to-all-start = ((f32[128,32,128]{2,1,0:T(8,128)}), f32[128,32,128]{2,1,0:T(8,128)}, u32[]{:S(2)}, u32[]{:S(2)}) async-start(f32[128,32,128]{2,1,0:T(8,128)} %stack.8), calls=%async_computation | async-start | bytes 4194304 | tf_op jit(solution)/shard_map/while/body/eval_jaxpr/all_to_all | solution.py:194
  165.6 16.2 %all-to-all-done = f32[128,32,128]{2,1,0:T(8,128)} async-done(((f32[128,32,128]{2,1,0:T(8,128)}), f32[128,32,128]{2,1,0:T(8,128)}, u32[]{:S(2)}, u32[]{:S(2)}) %all-to-all-start) | async-done | bytes 2097184 | tf_op jit(solution)/shard_map/while/body/eval_jaxpr/all_to_all | solution.py:194
  184.9 5.6 %fusion.99 = f32[4096,256]{1,0:T(8,128)S(1)} fusion(f32[4096,256]{1,0:T(8,128)} %bitcast.75, f32[4096,128]{1,0:T(8,128)S(1)} %get-tuple-element.720, f32[4096]{0:T(1024)S(1)} %broadcast_multiply_fusion.10, f32[256,128]{1,0:T(8,128)S(1)} %gather_fusion.1, f32[256]{0:T(256)S(1)} %broadcast_multiply_fusion.8), kind=kOutput, calls=%fused_computation.20.clone.1 | convolution fusion | flops 1613266944 | bytes 10634240 | tf_op jit(solution)/shard_map/while/body/eval_jaxpr/dot_general | solution.py:70
  190.5 3.6 fusion.100
  194.4 4.6 %fusion.102 = (f32[4096]{0:T(1024)S(1)}, f32[4096,128]{1,0:T(8,128)S(1)}) fusion(f32[256,128]{1,0:T(8,128)S(1)} %gather_fusion.1, f32[256]{0:T(256)S(1)} %broadcast_multiply_fusion.8, f32[4096,256]{1,0:T(8,128)S(1)} %fusion.99, f32[256]{0:T(256)S(1)} %get-tuple-element.693, f32[4096,128]{1,0:T(8,128)S(1)} %get-tuple-element.720, ...), kind=kOutput, calls=%fused_computation.162.clone.1 | convolution fusion | flops 1613787136 | bytes 8570880 | tf_op jit(solution)/shard_map/while/body/eval_jaxpr/dot_general | solution.py:77
  200.6 5.8 %all-to-all-start = ((f32[128,32,128]{2,1,0:T(8,128)}), f32[128,32,128]{2,1,0:T(8,128)}, u32[]{:S(2)}, u32[]{:S(2)}) async-start(f32[128,32,128]{2,1,0:T(8,128)} %stack.8), calls=%async_computation | async-start | bytes 4194304 | tf_op jit(solution)/shard_map/while/body/eval_jaxpr/all_to_all | solution.py:194
  220.1 16.3 %all-to-all-done = f32[128,32,128]{2,1,0:T(8,128)} async-done(((f32[128,32,128]{2,1,0:T(8,128)}), f32[128,32,128]{2,1,0:T(8,128)}, u32[]{:S(2)}, u32[]{:S(2)}) %all-to-all-start) | async-done | bytes 2097184 | tf_op jit(solution)/shard_map/while/body/eval_jaxpr/all_to_all | solution.py:194
  239.5 5.6 %fusion.99 = f32[4096,256]{1,0:T(8,128)S(1)} fusion(f32[4096,256]{1,0:T(8,128)} %bitcast.75, f32[4096,128]{1,0:T(8,128)S(1)} %get-tuple-element.720, f32[4096]{0:T(1024)S(1)} %broadcast_multiply_fusion.10, f32[256,128]{1,0:T(8,128)S(1)} %gather_fusion.1, f32[256]{0:T(256)S(1)} %broadcast_multiply_fusion.8), kind=kOutput, calls=%fused_computation.20.clone.1 | convolution fusion | flops 1613266944 | bytes 10634240 | tf_op jit(solution)/shard_map/while/body/eval_jaxpr/dot_general | solution.py:70
  245.1 3.6 fusion.100
  249.0 4.6 %fusion.102 = (f32[4096]{0:T(1024)S(1)}, f32[4096,128]{1,0:T(8,128)S(1)}) fusion(f32[256,128]{1,0:T(8,128)S(1)} %gather_fusion.1, f32[256]{0:T(256)S(1)} %broadcast_multiply_fusion.8, f32[4096,256]{1,0:T(8,128)S(1)} %fusion.99, f32[256]{0:T(256)S(1)} %get-tuple-element.693, f32[4096,128]{1,0:T(8,128)S(1)} %get-tuple-element.720, ...), kind=kOutput, calls=%fused_computation.162.clone.1 | convolution fusion | flops 1613787136 | bytes 8570880 | tf_op jit(solution)/shard_map/while/body/eval_jaxpr/dot_general | solution.py:77
  255.3 5.8 %all-to-all-start = ((f32[128,32,128]{2,1,0:T(8,128)}), f32[128,32,128]{2,1,0:T(8,128)}, u32[]{:S(2)}, u32[]{:S(2)}) async-start(f32[128,32,128]{2,1,0:T(8,128)} %stack.8), calls=%async_computation | async-start | bytes 4194304 | tf_op jit(solution)/shard_map/while/body/eval_jaxpr/all_to_all | solution.py:194
  274.7 16.3 %all-to-all-done = f32[128,32,128]{2,1,0:T(8,128)} async-done(((f32[128,32,128]{2,1,0:T(8,128)}), f32[128,32,128]{2,1,0:T(8,128)}, u32[]{:S(2)}, u32[]{:S(2)}) %all-to-all-start) | async-done | bytes 2097184 | tf_op jit(solution)/shard_map/while/body/eval_jaxpr/all_to_all | solution.py:194
  294.2 5.6 %fusion.99 = f32[4096,256]{1,0:T(8,128)S(1)} fusion(f32[4096,256]{1,0:T(8,128)} %bitcast.75, f32[4096,128]{1,0:T(8,128)S(1)} %get-tuple-element.720, f32[4096]{0:T(1024)S(1)} %broadcast_multiply_fusion.10, f32[256,128]{1,0:T(8,128)S(1)} %gather_fusion.1, f32[256]{0:T(256)S(1)} %broadcast_multiply_fusion.8), kind=kOutput, calls=%fused_computation.20.clone.1 | convolution fusion | flops 1613266944 | bytes 10634240 | tf_op jit(solution)/shard_map/while/body/eval_jaxpr/dot_general | solution.py:70
  299.7 3.6 fusion.100
  303.6 4.6 %fusion.102 = (f32[4096]{0:T(1024)S(1)}, f32[4096,128]{1,0:T(8,128)S(1)}) fusion(f32[256,128]{1,0:T(8,128)S(1)} %gather_fusion.1, f32[256]{0:T(256)S(1)} %broadcast_multiply_fusion.8, f32[4096,256]{1,0:T(8,128)S(1)} %fusion.99, f32[256]{0:T(256)S(1)} %get-tuple-element.693, f32[4096,128]{1,0:T(8,128)S(1)} %get-tuple-element.720, ...), kind=kOutput, calls=%fused_computation.162.clone.1 | convolution fusion | flops 1613787136 | bytes 8570880 | tf_op jit(solution)/shard_map/while/body/eval_jaxpr/dot_general | solution.py:77
  309.9 5.8 %all-to-all-start = ((f32[128,32,128]{2,1,0:T(8,128)}), f32[128,32,128]{2,1,0:T(8,128)}, u32[]{:S(2)}, u32[]{:S(2)}) async-start(f32[128,32,128]{2,1,0:T(8,128)} %stack.8), calls=%async_computation | async-start | bytes 4194304 | tf_op jit(solution)/shard_map/while/body/eval_jaxpr/all_to_all | solution.py:194
  329.3 16.3 %all-to-all-done = f32[128,32,128]{2,1,0:T(8,128)} async-done(((f32[128,32,128]{2,1,0:T(8,128)}), f32[128,32,128]{2,1,0:T(8,128)}, u32[]{:S(2)}, u32[]{:S(2)}) %all-to-all-start) | async-done | bytes 2097184 | tf_op jit(solution)/shard_map/while/body/eval_jaxpr/all_to_all | solution.py:194
  348.8 5.6 %fusion.99 = f32[4096,256]{1,0:T(8,128)S(1)} fusion(f32[4096,256]{1,0:T(8,128)} %bitcast.75, f32[4096,128]{1,0:T(8,128)S(1)} %get-tuple-element.720, f32[4096]{0:T(1024)S(1)} %broadcast_multiply_fusion.10, f32[256,128]{1,0:T(8,128)S(1)} %gather_fusion.1, f32[256]{0:T(256)S(1)} %broadcast_multiply_fusion.8), kind=kOutput, calls=%fused_computation.20.clone.1 | convolution fusion | flops 1613266944 | bytes 10634240 | tf_op jit(solution)/shard_map/while/body/eval_jaxpr/dot_general | solution.py:70
  354.4 3.6 fusion.100
  358.3 4.6 %fusion.102 = (f32[4096]{0:T(1024)S(1)}, f32[4096,128]{1,0:T(8,128)S(1)}) fusion(f32[256,128]{1,0:T(8,128)S(1)} %gather_fusion.1, f32[256]{0:T(256)S(1)} %broadcast_multiply_fusion.8, f32[4096,256]{1,0:T(8,128)S(1)} %fusion.99, f32[256]{0:T(256)S(1)} %get-tuple-element.693, f32[4096,128]{1,0:T(8,128)S(1)} %get-tuple-element.720, ...), kind=kOutput, calls=%fused_computation.162.clone.1 | convolution fusion | flops 1613787136 | bytes 8570880 | tf_op jit(solution)/shard_map/while/body/eval_jaxpr/dot_general | solution.py:77
  (210 shorter events, 105.3 us)
Async XLA Ops:
  1.3 113.3 %collective-permute-start.2 = (f32[8,16,1,128]{3,2,1,0:T(1,128)S(1)}, f32[8,16,1,128]{3,2,1,0:T(1,128)S(1)}, u32[]{:S(2)}, u32[]{:S(2)}) collective-permute-start(f32[8,16,1,128]{3,2,1,0:T(1,128)S(1)} %get-tuple-element.577), channel_id=1, source_target_pairs={{1,0},{2,1},{3,2},{4,3},{5,4},{6,5},{7,6},{9,8},{10,9},{11,10},{12... | collective-permute-start | bytes 196616 | tf_op jit(solution)/shard_map/ppermute | solution.py:21
  4.6 110.0 %collective-permute-start.3 = (f32[8,16,1,128]{3,2,1,0:T(1,128)S(1)}, f32[8,16,1,128]{3,2,1,0:T(1,128)S(1)}, u32[]{:S(2)}, u32[]{:S(2)}) collective-permute-start(f32[8,16,1,128]{3,2,1,0:T(1,128)S(1)} %get-tuple-element.578), channel_id=1, source_target_pairs={{0,1},{1,2},{2,3},{3,4},{4,5},{5,6},{6,7},{8,9},{9,10},{10,11},{11... | collective-permute-start | bytes 196616 | tf_op jit(solution)/shard_map/ppermute | solution.py:19
  9.2 105.5 %collective-permute-start.1 = (f32[8,1,32,128]{3,2,1,0:T(8,128)S(1)}, f32[8,1,32,128]{3,2,1,0:T(8,128)S(1)}, u32[]{:S(2)}, u32[]{:S(2)}) collective-permute-start(f32[8,1,32,128]{3,2,1,0:T(8,128)S(1)} %get-tuple-element.575), channel_id=1, source_target_pairs={{0,8},{8,16},{16,24},{24,32},{32,40},{40,48},{48,56},{56,64},{64,7... | collective-permute-start | bytes 393224 | tf_op jit(solution)/shard_map/ppermute | solution.py:19
  10.5 104.2 %collective-permute-start = (f32[8,1,32,128]{3,2,1,0:T(8,128)S(1)}, f32[8,1,32,128]{3,2,1,0:T(8,128)S(1)}, u32[]{:S(2)}, u32[]{:S(2)}) collective-permute-start(f32[8,1,32,128]{3,2,1,0:T(8,128)S(1)} %get-tuple-element.576), channel_id=1, source_target_pairs={{8,0},{16,8},{24,16},{32,24},{40,32},{48,40},{56,48},{64,56},{72,6... | collective-permute-start | bytes 393224 | tf_op jit(solution)/shard_map/ppermute | solution.py:21
  30.5 4.6 %copy-start.3 = (s32[1024]{0:T(1024)S(1)}, s32[1024]{0:T(1024)}, u32[]{:S(2)}) copy-start(s32[1024]{0:T(1024)} %param.20) | copy-start | bytes 12292
  30.5 4.6 %copy-start.7 = (s32[1024]{0:T(1024)S(1)}, s32[1024]{0:T(1024)}, u32[]{:S(2)}) copy-start(s32[1024]{0:T(1024)} %param.18) | copy-start | bytes 12292
  30.5 5.0 %copy-start.8 = (f32[1,1,32]{2,1,0:T(1,128)S(1)}, f32[1,1,32]{2,1,0:T(1,128)}, u32[]{:S(2)}) copy-start(f32[1,1,32]{2,1,0:T(1,128)} %param.22) | copy-start | bytes 388
  30.5 5.2 %copy-start.9 = (f32[1,1,32]{2,1,0:T(1,128)S(1)}, f32[1,1,32]{2,1,0:T(1,128)}, u32[]{:S(2)}) copy-start(f32[1,1,32]{2,1,0:T(1,128)} %param.23) | copy-start | bytes 388
  107.7 7.0 %copy-start.4 = (f32[4,16,32]{2,1,0:T(8,128)S(1)}, f32[4,16,32]{2,1,0:T(8,128)}, u32[]{:S(2)}) copy-start(f32[4,16,32]{2,1,0:T(8,128)} %param.14) | copy-start | bytes 24580
  107.7 7.0 %copy-start.5 = (f32[4,16,32]{2,1,0:T(8,128)S(1)}, f32[4,16,32]{2,1,0:T(8,128)}, u32[]{:S(2)}) copy-start(f32[4,16,32]{2,1,0:T(8,128)} %param.15) | copy-start | bytes 24580
  107.7 7.1 %copy-start.6 = (f32[4,16,32]{2,1,0:T(8,128)S(1)}, f32[4,16,32]{2,1,0:T(8,128)}, u32[]{:S(2)}) copy-start(f32[4,16,32]{2,1,0:T(8,128)} %param.16) | copy-start | bytes 24580
  107.7 7.1 %copy-start.2 = (f32[8,16,32,128]{3,2,1,0:T(8,128)S(1)}, f32[8,16,32,128]{3,2,1,0:T(8,128)}, u32[]{:S(2)}) copy-start(f32[8,16,32,128]{3,2,1,0:T(8,128)} %param.13) | copy-start | bytes 6291460
  117.0 11.8 %collective-permute-start.5 = (f32[8,1,32,128]{3,2,1,0:T(8,128)S(1)}, f32[8,1,32,128]{3,2,1,0:T(8,128)S(1)}, u32[]{:S(2)}, u32[]{:S(2)}) collective-permute-start(f32[8,1,32,128]{3,2,1,0:T(8,128)S(1)} %get-tuple-element.571), channel_id=1, source_target_pairs={{0,8},{8,16},{16,24},{24,32},{32,40},{40,48},{48,56},{56,64},{64,7... | collective-permute-start | bytes 393224 | tf_op jit(solution)/shard_map/ppermute | solution.py:19
  117.4 11.5 %collective-permute-start.4 = (f32[8,1,32,128]{3,2,1,0:T(8,128)S(1)}, f32[8,1,32,128]{3,2,1,0:T(8,128)S(1)}, u32[]{:S(2)}, u32[]{:S(2)}) collective-permute-start(f32[8,1,32,128]{3,2,1,0:T(8,128)S(1)} %get-tuple-element.572), channel_id=1, source_target_pairs={{8,0},{16,8},{24,16},{32,24},{40,32},{48,40},{56,48},{64,56},{72,6... | collective-permute-start | bytes 393224 | tf_op jit(solution)/shard_map/ppermute | solution.py:21
  122.0 5.6 %collective-permute-start.6 = (f32[8,16,1,128]{3,2,1,0:T(1,128)S(1)}, f32[8,16,1,128]{3,2,1,0:T(1,128)S(1)}, u32[]{:S(2)}, u32[]{:S(2)}) collective-permute-start(f32[8,16,1,128]{3,2,1,0:T(1,128)S(1)} %get-tuple-element.573), channel_id=1, source_target_pairs={{1,0},{2,1},{3,2},{4,3},{5,4},{6,5},{7,6},{9,8},{10,9},{11,10},{12... | collective-permute-start | bytes 196616 | tf_op jit(solution)/shard_map/ppermute | solution.py:21
  125.1 3.8 %collective-permute-start.7 = (f32[8,16,1,128]{3,2,1,0:T(1,128)S(1)}, f32[8,16,1,128]{3,2,1,0:T(1,128)S(1)}, u32[]{:S(2)}, u32[]{:S(2)}) collective-permute-start(f32[8,16,1,128]{3,2,1,0:T(1,128)S(1)} %get-tuple-element.574), channel_id=1, source_target_pairs={{0,1},{1,2},{2,3},{3,4},{4,5},{5,6},{6,7},{8,9},{9,10},{10,11},{11... | collective-permute-start | bytes 196616 | tf_op jit(solution)/shard_map/ppermute | solution.py:19
  131.0 11.2 %copy-start = (s32[1024]{0:T(1024)S(1)}, s32[1024]{0:T(1024)}, u32[]{:S(2)}) copy-start(s32[1024]{0:T(1024)} %param.19) | copy-start | bytes 12292
  132.3 9.9 %all-to-all-start.1 = ((f32[16,2,128]{2,1,0:T(2,128)}), f32[16,2,128]{2,1,0:T(2,128)S(1)}, u32[]{:S(2)}, u32[]{:S(2)}) async-start(f32[16,2,128]{2,1,0:T(2,128)} %broadcast_select_fusion), calls=%async_computation.1 | async-start | bytes 32768 | tf_op jit(solution)/shard_map/all_to_all | solution.py:174
  143.8 38.0 %all-to-all-start = ((f32[128,32,128]{2,1,0:T(8,128)}), f32[128,32,128]{2,1,0:T(8,128)}, u32[]{:S(2)}, u32[]{:S(2)}) async-start(f32[128,32,128]{2,1,0:T(8,128)} %stack.8), calls=%async_computation | async-start | bytes 4194304 | tf_op jit(solution)/shard_map/while/body/eval_jaxpr/all_to_all | solution.py:194
  200.6 35.8 %all-to-all-start = ((f32[128,32,128]{2,1,0:T(8,128)}), f32[128,32,128]{2,1,0:T(8,128)}, u32[]{:S(2)}, u32[]{:S(2)}) async-start(f32[128,32,128]{2,1,0:T(8,128)} %stack.8), calls=%async_computation | async-start | bytes 4194304 | tf_op jit(solution)/shard_map/while/body/eval_jaxpr/all_to_all | solution.py:194
  255.3 35.8 %all-to-all-start = ((f32[128,32,128]{2,1,0:T(8,128)}), f32[128,32,128]{2,1,0:T(8,128)}, u32[]{:S(2)}, u32[]{:S(2)}) async-start(f32[128,32,128]{2,1,0:T(8,128)} %stack.8), calls=%async_computation | async-start | bytes 4194304 | tf_op jit(solution)/shard_map/while/body/eval_jaxpr/all_to_all | solution.py:194
  309.9 35.8 %all-to-all-start = ((f32[128,32,128]{2,1,0:T(8,128)}), f32[128,32,128]{2,1,0:T(8,128)}, u32[]{:S(2)}, u32[]{:S(2)}) async-start(f32[128,32,128]{2,1,0:T(8,128)} %stack.8), calls=%async_computation | async-start | bytes 4194304 | tf_op jit(solution)/shard_map/while/body/eval_jaxpr/all_to_all | solution.py:194
  362.9 1.3 copy-start.1
